TPU v7x, 128 devices: a whole 4x4x4 slice. The times are simulated.
128 devices in a mesh: wa: 16 (over x, z), ha: 8 (over y, core).
Axes of the slice: x: 4, y: 4, z: 4, core: 2. Of those that a mesh axis runs over, the one named last changes fastest.
Arguments:
- tokens: bfloat16 [512, 16384], P('ha', 'wa'), may hold values from -100 to 100, as said below
- norm_gain: float32 [16384], P('wa'), may hold values from 0.5 to 1.5
- gate_weight: bfloat16 [16384, 26624], P('wa', 'ha'), may hold values from -0.046875 to 0.046875
- up_weight: bfloat16 [16384, 26624], P('wa', 'ha'), may hold values from -0.046875 to 0.046875
- down_weight: bfloat16 [26624, 16384], P('ha', 'wa'), may hold values from -0.0390625 to 0.0390625
Outputs:
- mixed: bfloat16 [512, 16384], P('ha', 'wa')
Inputs may be any that keep to these rules, and one draw needn't show every extreme that they name: `tokens`: real-valued activations.
All inputs are finite; a program needn't handle non-finite values.
Results may differ from a plain program's by a relative error of at most 0.0064.
Values may be sent and summed in bfloat16 or wider, within the bound.
A program may use at most 128 MiB of HBM per device.

v0:
```python
import jax
import jax.numpy as jnp
from jax import lax
from jax.sharding import PartitionSpec as P


def apply_norm(own_values, squares, norm_gain):
    model_width = own_values.shape[1] * lax.axis_size("wa")
    mean_square = squares[:, None] / model_width
    return (own_values * lax.rsqrt(mean_square + 1e-05) * norm_gain[None, :]).astype(jnp.bfloat16)


def activate(summed, hidden_width):
    gate = summed[:, :hidden_width]
    up = summed[:, hidden_width:]
    return (jax.nn.silu(gate) * up).astype(jnp.bfloat16)


def body(tokens, norm_gain, gate_weight, up_weight, down_weight):
    gathered = lax.all_gather(tokens, "ha", axis=0, tiled=True)
    own_values = gathered.astype(jnp.float32)
    squares = lax.psum(jnp.sum(own_values * own_values, axis=1), "wa")
    normed = apply_norm(own_values, squares, norm_gain)
    hidden_width = gate_weight.shape[1]
    gate_part = jnp.dot(normed, gate_weight, preferred_element_type=jnp.float32)
    up_part = jnp.dot(normed, up_weight, preferred_element_type=jnp.float32)
    summed = lax.psum_scatter(
        jnp.concatenate([gate_part, up_part], axis=1), "wa", scatter_dimension=0, tiled=True
    )
    hidden = activate(summed, hidden_width)
    partial_out = jnp.dot(
        lax.all_gather(hidden, "wa", axis=0, tiled=True),
        down_weight,
        preferred_element_type=jnp.float32,
    )
    mixed_out = lax.psum_scatter(partial_out, "ha", scatter_dimension=0, tiled=True)
    return mixed_out.astype(jnp.bfloat16)


def solution(mesh):
    placed = (P("ha", "wa"), P("wa"), P("wa", "ha"), P("wa", "ha"), P("ha", "wa"))
    return jax.shard_map(body, mesh=mesh, in_specs=placed, out_specs=P("ha", "wa"), check_vma=False)
```

profile of v0, /device:TPU:0, one launch (start us, length us, event | category | flops | bytes accessed | tf_op | source)
XLA Modules:
  0.0 285.8 jit_solution(6064925622431984980)
XLA Ops:
  6.5 0.0 all-gather.3.cloned.1.call-start
  6.5 0.7 all-gather.3.cloned.1.call-update
  7.3 0.0 reduce-scatter.3.cloned.1.call-start
  7.3 27.6 %all-gather.3.cloned.1.call-done = bf16[512,1024]{1,0:T(8,128)(2,1)} async-done(((bf16[64,1024]{1,0:T(8,128)(2,1)}), bf16[512,1024]{1,0:T(8,128)(2,1)}) %all-gather.3.cloned.1.call-update) | async-done | bytes 1048592 | tf_op jit(solution)/shard_map/all_gather | solution.py:20
  34.9 0.0 slice-start
  34.9 1.7 fusion
  36.6 40.5 %psum.7 = f32[512]{0:T(512)S(1)} all-reduce(f32[512]{0:T(512)S(1)} %fusion), channel_id=1, replica_groups=mesh['wa'=16,'ha'=8] {'wa'}, use_global_device_ids=true, to_apply=%region_1.0 | all-reduce | flops 512 | bytes 4096 | tf_op jit(solution)/shard_map/psum | solution.py:22
  77.1 0.0 copy-start
  77.1 0.0 slice-start.1
  77.1 0.0 copy-start.1
  77.1 6.7 %fusion.4 = f32[512,3328]{1,0:T(8,128)S(1)} fusion(bf16[1024,3328]{1,0:T(8,128)(2,1)} %param.8, bf16[512,1024]{1,0:T(8,128)(2,1)} %all-gather.3.cloned.1.call-done, f32[1024]{0:T(1024)} %param.6, f32[512]{0:T(512)S(1)} %add_rsqrt_fusion), kind=kOutput, calls=%fused_computation.8 | convolution fusion | flops 3491758080 | bytes 14686208 | tf_op jit(solution)/shard_map/dot_general | solution.py:26
  83.9 0.0 slice-done
  83.9 0.0 copy-done
  83.9 0.0 slice-done.1
  83.9 0.0 copy-done.1
  83.9 3.8 %fusion.6 = f32[512,3328]{1,0:T(8,128)S(1)} fusion(bf16[1024,3328]{1,0:T(8,128)(2,1)S(1)} %bitcast.5, bf16[512,1024]{1,0:T(8,128)(2,1)S(1)} %copy-done, f32[1024]{0:T(1024)S(1)} %copy-done.1, f32[512]{0:T(512)S(1)} %add_rsqrt_fusion), kind=kOutput, calls=%fused_computation.9 | convolution fusion | flops 3491758080 | bytes 14686208 | tf_op jit(solution)/shard_map/dot_general | solution.py:25
  87.8 5.4 %pad_maximum_fusion = f32[512,6656]{1,0:T(8,128)} fusion(f32[512,3328]{1,0:T(8,128)S(1)} %fusion.4, f32[512,3328]{1,0:T(8,128)S(1)} %fusion.6), kind=kLoop, calls=%fused_computation | loop fusion | flops 3407872 | bytes 27262976 | tf_op jit(solution)/shard_map/concatenate | solution.py:28
  93.2 0.0 reduce-scatter.3.cloned.1.call-update
  93.2 0.0 all-gather.5.cloned.1.call-start
  93.3 92.7 %reduce-scatter.3.cloned.1.call-done = f32[32,6656]{1,0:T(8,128)} async-done(((f32[512,6656]{1,0:T(8,128)}), f32[32,6656]{1,0:T(8,128)}) %reduce-scatter.3.cloned.1.call-update) | async-done | bytes 851984 | tf_op jit(solution)/shard_map/reduce_scatter | solution.py:27
  185.9 1.9 fusion.3
  187.9 0.0 all-gather.5.cloned.1.call-update
  187.9 0.0 reduce-scatter.5.cloned.1.call-start
  187.9 48.1 %all-gather.5.cloned.1.call-done = bf16[512,3328]{1,0:T(8,128)(2,1)} async-done(((bf16[32,3328]{1,0:T(8,128)(2,1)}), bf16[512,3328]{1,0:T(8,128)(2,1)}) %all-gather.5.cloned.1.call-update) | async-done | bytes 3407888 | tf_op jit(solution)/shard_map/all_gather | solution.py:32
  236.1 9.0 %fusion.8 = f32[512,1024]{1,0:T(8,128)} fusion(bf16[512,3328]{1,0:T(8,128)(2,1)} %all-gather.5.cloned.1.call-done, bf16[3328,1024]{1,0:T(8,128)(2,1)} %param.9), kind=kOutput, calls=%fused_computation.11 | convolution fusion | flops 3489660928 | bytes 12320768 | tf_op jit(solution)/shard_map/dot_general | solution.py:31
  245.1 0.0 reduce-scatter.5.cloned.1.call-update
  245.1 32.6 %reduce-scatter.5.cloned.1.call-done = f32[64,1024]{1,0:T(8,128)} async-done(((f32[512,1024]{1,0:T(8,128)}), f32[64,1024]{1,0:T(8,128)}) %reduce-scatter.5.cloned.1.call-update) | async-done | bytes 262160 | tf_op jit(solution)/shard_map/reduce_scatter | solution.py:36
  277.7 1.6 convert_element_type.15
  (2 shorter events, 0.0 us)
Async XLA Ops:
  6.5 28.4 %all-gather.3.cloned.1.call-start = ((), (), s32[]{:S(2)}) async-start(), calls=%async_computation.2 | async-start | bytes 1179648 | tf_op jit(solution)/shard_map/all_gather | solution.py:20
  7.3 178.7 %reduce-scatter.3.cloned.1.call-start = ((), (), s32[]{:S(2)}) async-start(), calls=%async_computation.3 | async-start | bytes 14483456 | tf_op jit(solution)/shard_map/reduce_scatter | solution.py:27
  34.9 48.9 %slice-start = ((s8[6815744]{0:T(1024)(128)(4,1)}), s8[2621440]{0:T(1024)(128)(4,1)S(1)}, s32[]{:S(2)}) async-start(s8[6815744]{0:T(1024)(128)(4,1)} %bitcast.4), calls=%async_computation.6 | async-start | bytes 5242880
  77.1 6.8 %copy-start = (bf16[512,1024]{1,0:T(8,128)(2,1)S(1)}, bf16[512,1024]{1,0:T(8,128)(2,1)}, u32[]{:S(2)}) copy-start(bf16[512,1024]{1,0:T(8,128)(2,1)} %all-gather.3.cloned.1.call-done) | copy-start | bytes 3145732
  77.1 6.8 %slice-start.1 = ((s8[6815744]{0:T(1024)(128)(4,1)}), s8[4194304]{0:T(1024)(128)(4,1)S(1)}, s32[]{:S(2)}) async-start(s8[6815744]{0:T(1024)(128)(4,1)} %bitcast.4), calls=%async_computation.7 | async-start | bytes 8388608
  77.1 6.8 %copy-start.1 = (f32[1024]{0:T(1024)S(1)}, f32[1024]{0:T(1024)}, u32[]{:S(2)}) copy-start(f32[1024]{0:T(1024)} %param.6) | copy-start | bytes 12292
  93.2 142.8 %all-gather.5.cloned.1.call-start = ((), (), s32[]{:S(2)}) async-start(), calls=%async_computation.4 | async-start | bytes 3620864 | tf_op jit(solution)/shard_map/all_gather | solution.py:32
  187.9 89.8 %reduce-scatter.5.cloned.1.call-start = ((), (), s32[]{:S(2)}) async-start(), calls=%async_computation.5 | async-start | bytes 2359296 | tf_op jit(solution)/shard_map/reduce_scatter | solution.py:36
Sparse Core Ops, SparseCore 0:
  9.1 25.8 all-gather.2
  93.3 92.5 reduce-scatter.2
  188.4 47.6 all-gather.4
  245.2 32.3 reduce-scatter.4
where the time goes:
time: 286 us
  waiting for transfers between devices  202 us (71%)
  blocking collectives  40.5 us (14%)
  matrix products  19.5 us (7%)
  between operations  13.2 us (5%)
  other arithmetic  10.7 us (4%)
    reduce_scatter x1, waiting for transfers between devices, body(): lax.psum_scatter(jnp.concatenate([gate_part, up_part], axis=1), 'wa', sca...  92.7 us
    all_gather x1, waiting for transfers between devices, body(): lax.all_gather(hidden, 'wa', axis=0, tiled=True)  48.1 us
    psum x1, blocking collectives, body(): squares = lax.psum(jnp.sum(own_values * own_values, axis=1), 'wa')  40.5 us
    reduce_scatter x1, waiting for transfers between devices, body(): lax.psum_scatter(partial_out, 'ha', scatter_dimension=0, tiled=True)  32.6 us
    all_gather x1, waiting for transfers between devices, body(): gathered = lax.all_gather(tokens, 'ha', axis=0, tiled=True)  27.6 us
    dot_general x1, matrix products, body(): jnp.dot(lax.all_gather(hidden, 'wa', axis=0, tiled=True), down_weight, pr...  9 us
    dot_general x1, matrix products, body(): up_part = jnp.dot(normed, up_weight, preferred_element_type=jnp.float32)  6.72 us
  transfers between devices with their start and end apart: 4, of which 4 were waited for; matrix products, arithmetic and copies ran while one was open for 0% of the time, Pallas kernels for 0%

commit v1 on v0

--- a/solution.py
+++ b/solution.py
@@ -19,7 +19,7 @@
 def body(tokens, norm_gain, gate_weight, up_weight, down_weight):
     gathered = lax.all_gather(tokens, "ha", axis=0, tiled=True)
     own_values = gathered.astype(jnp.float32)
-    squares = lax.psum(jnp.sum(own_values * own_values, axis=1), "wa")
+    squares = jnp.sum(lax.all_gather(jnp.sum(own_values * own_values, axis=1), "wa"), axis=0)
     normed = apply_norm(own_values, squares, norm_gain)
     hidden_width = gate_weight.shape[1]
     gate_part = jnp.dot(normed, gate_weight, preferred_element_type=jnp.float32)

time: 286 us -> 273 us (0.955)
  blocking collectives: 40.5 us -> 23.5 us
  waiting for transfers between devices: 202 us -> 205 us
    psum x1 -> x0, blocking collectives: 40.5 us -> none  [body(): squares = lax.psum(jnp.sum(own_values * own_values, axis=1), 'wa')]
    all_gather x0 -> x1, blocking collectives: none -> 23.5 us  [body(): lax.all_gather(jnp.sum(own_values * own_values, axis=1), 'wa')]
    reduce_scatter x1, waiting for transfers between devices: 92.7 us -> 95.7 us  [body(): lax.psum_scatter(jnp.concatenate([gate_part, up_part], axis=1), 'wa', sca...]
where the time goes in v1:
time: 273 us
  waiting for transfers between devices  205 us (75%)
  blocking collectives  23.5 us (9%)
  matrix products  20.2 us (7%)
  between operations  13.2 us (5%)
  other arithmetic  10.7 us (4%)
    reduce_scatter x1, waiting for transfers between devices, body(): lax.psum_scatter(jnp.concatenate([gate_part, up_part], axis=1), 'wa', sca...  95.7 us
    all_gather x1, waiting for transfers between devices, body(): lax.all_gather(hidden, 'wa', axis=0, tiled=True)  48.1 us
    reduce_scatter x1, waiting for transfers between devices, body(): lax.psum_scatter(partial_out, 'ha', scatter_dimension=0, tiled=True)  32.6 us
    all_gather x1, waiting for transfers between devices, body(): gathered = lax.all_gather(tokens, 'ha', axis=0, tiled=True)  27.6 us
    all_gather x1, blocking collectives, body(): lax.all_gather(jnp.sum(own_values * own_values, axis=1), 'wa')  23.5 us
    dot_general x1, matrix products, body(): jnp.dot(lax.all_gather(hidden, 'wa', axis=0, tiled=True), down_weight, pr...  9 us
    dot_general x1, matrix products, body(): up_part = jnp.dot(normed, up_weight, preferred_element_type=jnp.float32)  7.42 us
  transfers between devices with their start and end apart: 4, of which 4 were waited for; matrix products, arithmetic and copies ran while one was open for 0% of the time, Pallas kernels for 0%

profile of v1, /device:TPU:0, one launch (start us, length us, event | category | flops | bytes accessed | tf_op | source)
XLA Modules:
  0.0 272.5 jit_solution(6042366554275755285)
XLA Ops:
  6.5 0.0 all-gather.5.cloned.1.call-start
  6.5 0.7 all-gather.5.cloned.1.call-update
  7.3 0.0 reduce-scatter.3.cloned.1.call-start
  7.3 27.6 %all-gather.5.cloned.1.call-done = bf16[512,1024]{1,0:T(8,128)(2,1)} async-done(((bf16[64,1024]{1,0:T(8,128)(2,1)}), bf16[512,1024]{1,0:T(8,128)(2,1)}) %all-gather.5.cloned.1.call-update) | async-done | bytes 1048592 | tf_op jit(solution)/shard_map/all_gather | solution.py:20
  34.9 0.0 slice-start
  34.9 1.7 fusion
  36.6 23.5 %all-gather.1 = f32[16,1,512]{2,1,0:T(1,128)S(1)} all-gather(f32[1,1,512]{2,1,0:T(1,128)S(1)} %bitcast.5), channel_id=2, replica_groups=mesh['wa'=16,'ha'=8] {'wa'}, dimensions={0}, use_global_device_ids=true | all-gather | bytes 34816 | tf_op jit(solution)/shard_map/all_gather | solution.py:22
  60.1 0.0 copy-start
  60.1 0.0 slice-start.1
  60.2 0.0 copy-start.1
  60.2 7.4 %fusion.4 = f32[512,3328]{1,0:T(8,128)S(1)} fusion(bf16[1024,3328]{1,0:T(8,128)(2,1)} %param.8, bf16[512,1024]{1,0:T(8,128)(2,1)} %all-gather.5.cloned.1.call-done, f32[1024]{0:T(1024)} %param.6, f32[512]{0:T(512)S(1)} %add_rsqrt_fusion), kind=kOutput, calls=%fused_computation.8 | convolution fusion | flops 3491758080 | bytes 14686208 | tf_op jit(solution)/shard_map/dot_general | solution.py:26
  67.6 0.0 slice-done
  67.6 0.0 copy-done
  67.6 0.0 slice-done.1
  67.6 0.0 copy-done.1
  67.6 3.8 %fusion.6 = f32[512,3328]{1,0:T(8,128)S(1)} fusion(bf16[1024,3328]{1,0:T(8,128)(2,1)S(1)} %bitcast.7, bf16[512,1024]{1,0:T(8,128)(2,1)S(1)} %copy-done, f32[1024]{0:T(1024)S(1)} %copy-done.1, f32[512]{0:T(512)S(1)} %add_rsqrt_fusion), kind=kOutput, calls=%fused_computation.9 | convolution fusion | flops 3491758080 | bytes 14686208 | tf_op jit(solution)/shard_map/dot_general | solution.py:25
  71.4 5.4 %pad_maximum_fusion = f32[512,6656]{1,0:T(8,128)} fusion(f32[512,3328]{1,0:T(8,128)S(1)} %fusion.4, f32[512,3328]{1,0:T(8,128)S(1)} %fusion.6), kind=kLoop, calls=%fused_computation | loop fusion | flops 3407872 | bytes 27262976 | tf_op jit(solution)/shard_map/concatenate | solution.py:28
  76.9 0.0 reduce-scatter.3.cloned.1.call-update
  76.9 0.0 all-gather.7.cloned.1.call-start
  77.0 95.7 %reduce-scatter.3.cloned.1.call-done = f32[32,6656]{1,0:T(8,128)} async-done(((f32[512,6656]{1,0:T(8,128)}), f32[32,6656]{1,0:T(8,128)}) %reduce-scatter.3.cloned.1.call-update) | async-done | bytes 851984 | tf_op jit(solution)/shard_map/reduce_scatter | solution.py:27
  172.6 1.9 fusion.3
  174.6 0.0 all-gather.7.cloned.1.call-update
  174.6 0.0 reduce-scatter.5.cloned.1.call-start
  174.7 48.1 %all-gather.7.cloned.1.call-done = bf16[512,3328]{1,0:T(8,128)(2,1)} async-done(((bf16[32,3328]{1,0:T(8,128)(2,1)}), bf16[512,3328]{1,0:T(8,128)(2,1)}) %all-gather.7.cloned.1.call-update) | async-done | bytes 3407888 | tf_op jit(solution)/shard_map/all_gather | solution.py:32
  222.8 9.0 %fusion.8 = f32[512,1024]{1,0:T(8,128)} fusion(bf16[512,3328]{1,0:T(8,128)(2,1)} %all-gather.7.cloned.1.call-done, bf16[3328,1024]{1,0:T(8,128)(2,1)} %param.9), kind=kOutput, calls=%fused_computation.11 | convolution fusion | flops 3489660928 | bytes 12320768 | tf_op jit(solution)/shard_map/dot_general | solution.py:31
  231.8 0.0 reduce-scatter.5.cloned.1.call-update
  231.8 32.6 %reduce-scatter.5.cloned.1.call-done = f32[64,1024]{1,0:T(8,128)} async-done(((f32[512,1024]{1,0:T(8,128)}), f32[64,1024]{1,0:T(8,128)}) %reduce-scatter.5.cloned.1.call-update) | async-done | bytes 262160 | tf_op jit(solution)/shard_map/reduce_scatter | solution.py:36
  264.4 1.6 convert_element_type.15
  (3 shorter events, 0.1 us)
Async XLA Ops:
  6.5 28.4 %all-gather.5.cloned.1.call-start = ((), (), s32[]{:S(2)}) async-start(), calls=%async_computation.2 | async-start | bytes 1179648 | tf_op jit(solution)/shard_map/all_gather | solution.py:20
  7.3 165.4 %reduce-scatter.3.cloned.1.call-start = ((), (), s32[]{:S(2)}) async-start(), calls=%async_computation.3 | async-start | bytes 14483456 | tf_op jit(solution)/shard_map/reduce_scatter | solution.py:27
  34.9 32.7 %slice-start = ((s8[6815744]{0:T(1024)(128)(4,1)}), s8[2621440]{0:T(1024)(128)(4,1)S(1)}, s32[]{:S(2)}) async-start(s8[6815744]{0:T(1024)(128)(4,1)} %bitcast.6), calls=%async_computation.6 | async-start | bytes 5242880
  60.1 7.5 %copy-start = (bf16[512,1024]{1,0:T(8,128)(2,1)S(1)}, bf16[512,1024]{1,0:T(8,128)(2,1)}, u32[]{:S(2)}) copy-start(bf16[512,1024]{1,0:T(8,128)(2,1)} %all-gather.5.cloned.1.call-done) | copy-start | bytes 3145732
  60.1 7.5 %slice-start.1 = ((s8[6815744]{0:T(1024)(128)(4,1)}), s8[4194304]{0:T(1024)(128)(4,1)S(1)}, s32[]{:S(2)}) async-start(s8[6815744]{0:T(1024)(128)(4,1)} %bitcast.6), calls=%async_computation.7 | async-start | bytes 8388608
  60.2 7.5 %copy-start.1 = (f32[1024]{0:T(1024)S(1)}, f32[1024]{0:T(1024)}, u32[]{:S(2)}) copy-start(f32[1024]{0:T(1024)} %param.6) | copy-start | bytes 12292
  76.9 145.9 %all-gather.7.cloned.1.call-start = ((), (), s32[]{:S(2)}) async-start(), calls=%async_computation.4 | async-start | bytes 3620864 | tf_op jit(solution)/shard_map/all_gather | solution.py:32
  174.6 89.7 %reduce-scatter.5.cloned.1.call-start = ((), (), s32[]{:S(2)}) async-start(), calls=%async_computation.5 | async-start | bytes 2359296 | tf_op jit(solution)/shard_map/reduce_scatter | solution.py:36
Sparse Core Ops, SparseCore 0:
  9.1 25.8 all-gather.4
  77.0 95.5 reduce-scatter.2
  175.1 47.6 all-gather.6
  231.9 32.3 reduce-scatter.4

commit v2 on v0

--- a/solution.py
+++ b/solution.py
@@ -2,6 +2,14 @@
 import jax.numpy as jnp
 from jax import lax
 from jax.sharding import PartitionSpec as P
+
+
+def gather_from_all(array, axis, dim):
+    size = lax.axis_size(axis)
+    repeats = [size if d == dim else 1 for d in range(array.ndim)]
+    return lax.all_to_all(
+        jnp.tile(array, repeats), axis, split_axis=dim, concat_axis=dim, tiled=True
+    )
 
 
 def apply_norm(own_values, squares, norm_gain):
@@ -29,9 +37,7 @@
     )
     hidden = activate(summed, hidden_width)
     partial_out = jnp.dot(
-        lax.all_gather(hidden, "wa", axis=0, tiled=True),
-        down_weight,
-        preferred_element_type=jnp.float32,
+        gather_from_all(hidden, "wa", 0), down_weight, preferred_element_type=jnp.float32
     )
     mixed_out = lax.psum_scatter(partial_out, "ha", scatter_dimension=0, tiled=True)
     return mixed_out.astype(jnp.bfloat16)

time: 286 us -> 282 us (0.986)
  waiting for transfers between devices: 202 us -> 153 us
  blocking collectives: 40.5 us -> 86.5 us
    all_gather x1 -> x0, waiting for transfers between devices: 48.1 us -> none  [body(): lax.all_gather(hidden, 'wa', axis=0, tiled=True)]
    all_to_all x0 -> x1, blocking collectives: none -> 46 us  [gather_from_all(): lax.all_to_all(jnp.tile(array, repeats), axis, split_axis=dim, concat_axi...]
  transfers between devices with their start and end apart: 4 -> 3, of which waited for: 4 -> 3; matrix products, arithmetic and copies ran while one was open for 0% -> 0% of each run, Pallas kernels for 0% -> 0%
where the time goes in v2:
time: 282 us; the launch traced here: 281 us
  waiting for transfers between devices  153 us (54%)
  blocking collectives  86.5 us (31%)
  matrix products  18.5 us (7%)
  between operations  13.2 us (5%)
  other arithmetic  9.99 us (4%)
    reduce_scatter x1, waiting for transfers between devices, body(): lax.psum_scatter(jnp.concatenate([gate_part, up_part], axis=1), 'wa', sca...  92.7 us
    all_to_all x1, blocking collectives, gather_from_all(): lax.all_to_all(jnp.tile(array, repeats), axis, split_axis=dim, concat_axi...  46 us
    psum x1, blocking collectives, body(): squares = lax.psum(jnp.sum(own_values * own_values, axis=1), 'wa')  40.5 us
    reduce_scatter x1, waiting for transfers between devices, body(): lax.psum_scatter(partial_out, 'ha', scatter_dimension=0, tiled=True)  31.7 us
    all_gather x1, waiting for transfers between devices, body(): gathered = lax.all_gather(tokens, 'ha', axis=0, tiled=True)  27.6 us
    dot_general x1, matrix products, body(): jnp.dot(gather_from_all(hidden, 'wa', 0), down_weight, preferred_element_...  8 us
    dot_general x1, matrix products, body(): up_part = jnp.dot(normed, up_weight, preferred_element_type=jnp.float32)  6.72 us
  transfers between devices with their start and end apart: 3, of which 3 were waited for; matrix products, arithmetic and copies ran while one was open for 0% of the time, Pallas kernels for 0%

profile of v2, /device:TPU:0, one launch (start us, length us, event | category | flops | bytes accessed | tf_op | source)
XLA Modules:
  0.0 281.4 jit_solution(5446141623675686904)
XLA Ops:
  6.5 0.0 all-gather.2.cloned.1.call-start
  6.5 0.7 all-gather.2.cloned.1.call-update
  7.3 0.0 reduce-scatter.3.cloned.1.call-start
  7.3 27.6 %all-gather.2.cloned.1.call-done = bf16[512,1024]{1,0:T(8,128)(2,1)} async-done(((bf16[64,1024]{1,0:T(8,128)(2,1)}), bf16[512,1024]{1,0:T(8,128)(2,1)}) %all-gather.2.cloned.1.call-update) | async-done | bytes 1048592 | tf_op jit(solution)/shard_map/all_gather | solution.py:28
  34.9 0.0 slice-start
  34.9 1.7 fusion
  36.6 40.5 %psum.7 = f32[512]{0:T(512)S(1)} all-reduce(f32[512]{0:T(512)S(1)} %fusion), channel_id=1, replica_groups=mesh['wa'=16,'ha'=8] {'wa'}, use_global_device_ids=true, to_apply=%region_1.0 | all-reduce | flops 512 | bytes 4096 | tf_op jit(solution)/shard_map/psum | solution.py:30
  77.1 0.0 copy-start
  77.1 0.0 slice-start.1
  77.1 0.0 copy-start.1
  77.1 6.7 %fusion.4 = f32[512,3328]{1,0:T(8,128)S(1)} fusion(bf16[1024,3328]{1,0:T(8,128)(2,1)} %param.8, bf16[512,1024]{1,0:T(8,128)(2,1)} %all-gather.2.cloned.1.call-done, f32[1024]{0:T(1024)} %param.6, f32[512]{0:T(512)S(1)} %add_rsqrt_fusion), kind=kOutput, calls=%fused_computation.8 | convolution fusion | flops 3491758080 | bytes 14686208 | tf_op jit(solution)/shard_map/dot_general | solution.py:34
  83.9 0.0 slice-done
  83.9 0.0 copy-done
  83.9 0.0 slice-done.1
  83.9 0.0 copy-done.1
  83.9 3.8 %fusion.6 = f32[512,3328]{1,0:T(8,128)S(1)} fusion(bf16[1024,3328]{1,0:T(8,128)(2,1)S(1)} %bitcast.7, bf16[512,1024]{1,0:T(8,128)(2,1)S(1)} %copy-done, f32[1024]{0:T(1024)S(1)} %copy-done.1, f32[512]{0:T(512)S(1)} %add_rsqrt_fusion), kind=kOutput, calls=%fused_computation.9 | convolution fusion | flops 3491758080 | bytes 14686208 | tf_op jit(solution)/shard_map/dot_general | solution.py:33
  87.8 5.5 %pad_maximum_fusion = f32[512,6656]{1,0:T(8,128)} fusion(f32[512,3328]{1,0:T(8,128)S(1)} %fusion.4, f32[512,3328]{1,0:T(8,128)S(1)} %fusion.6), kind=kLoop, calls=%fused_computation | loop fusion | flops 3407872 | bytes 27262976 | tf_op jit(solution)/shard_map/concatenate | solution.py:36
  93.2 0.0 reduce-scatter.3.cloned.1.call-update
  93.2 0.0 reduce-scatter.5.cloned.1.call-start
  93.3 92.7 %reduce-scatter.3.cloned.1.call-done = f32[32,6656]{1,0:T(8,128)} async-done(((f32[512,6656]{1,0:T(8,128)}), f32[32,6656]{1,0:T(8,128)}) %reduce-scatter.3.cloned.1.call-update) | async-done | bytes 851984 | tf_op jit(solution)/shard_map/reduce_scatter | solution.py:35
  185.9 1.3 fusion.3
  187.2 0.3 tile.2
  187.5 46.0 %all_to_all.9 = bf16[16,32,3328]{2,1,0:T(8,128)(2,1)S(1)} all-to-all(bf16[16,32,3328]{2,1,0:T(8,128)(2,1)S(1)} %tile.2), channel_id=1, replica_groups=mesh['wa'=16,'ha'=8] {'wa'}, dimensions={0} | all-to-all | bytes 6815744 | tf_op jit(solution)/shard_map/all_to_all | solution.py:10
  233.5 8.0 %fusion.8 = f32[512,1024]{1,0:T(8,128)} fusion(bf16[512,3328]{1,0:T(8,128)(2,1)S(1)} %bitcast.5, bf16[3328,1024]{1,0:T(8,128)(2,1)} %param.9), kind=kOutput, calls=%fused_computation.11 | convolution fusion | flops 3489660928 | bytes 12320768 | tf_op jit(solution)/shard_map/dot_general | solution.py:39
  241.5 0.0 reduce-scatter.5.cloned.1.call-update
  241.6 31.7 %reduce-scatter.5.cloned.1.call-done = f32[64,1024]{1,0:T(8,128)} async-done(((f32[512,1024]{1,0:T(8,128)}), f32[64,1024]{1,0:T(8,128)}) %reduce-scatter.5.cloned.1.call-update) | async-done | bytes 262160 | tf_op jit(solution)/shard_map/reduce_scatter | solution.py:42
  273.3 1.6 convert_element_type.15
  (2 shorter events, 0.0 us)
Async XLA Ops:
  6.5 28.4 %all-gather.2.cloned.1.call-start = ((), (), s32[]{:S(2)}) async-start(), calls=%async_computation.3 | async-start | bytes 1179648 | tf_op jit(solution)/shard_map/all_gather | solution.py:28
  7.3 178.7 %reduce-scatter.3.cloned.1.call-start = ((), (), s32[]{:S(2)}) async-start(), calls=%async_computation.4 | async-start | bytes 14483456 | tf_op jit(solution)/shard_map/reduce_scatter | solution.py:35
  34.9 48.9 %slice-start = ((s8[6815744]{0:T(1024)(128)(4,1)}), s8[2621440]{0:T(1024)(128)(4,1)S(1)}, s32[]{:S(2)}) async-start(s8[6815744]{0:T(1024)(128)(4,1)} %bitcast.6), calls=%async_computation.6 | async-start | bytes 5242880
  77.1 6.8 %copy-start = (bf16[512,1024]{1,0:T(8,128)(2,1)S(1)}, bf16[512,1024]{1,0:T(8,128)(2,1)}, u32[]{:S(2)}) copy-start(bf16[512,1024]{1,0:T(8,128)(2,1)} %all-gather.2.cloned.1.call-done) | copy-start | bytes 3145732
  77.1 6.8 %slice-start.1 = ((s8[6815744]{0:T(1024)(128)(4,1)}), s8[4194304]{0:T(1024)(128)(4,1)S(1)}, s32[]{:S(2)}) async-start(s8[6815744]{0:T(1024)(128)(4,1)} %bitcast.6), calls=%async_computation.7 | async-start | bytes 8388608
  77.1 6.8 %copy-start.1 = (f32[1024]{0:T(1024)S(1)}, f32[1024]{0:T(1024)}, u32[]{:S(2)}) copy-start(f32[1024]{0:T(1024)} %param.6) | copy-start | bytes 12292
  93.2 180.1 %reduce-scatter.5.cloned.1.call-start = ((), (), s32[]{:S(2)}) async-start(), calls=%async_computation.5 | async-start | bytes 2359296 | tf_op jit(solution)/shard_map/reduce_scatter | solution.py:42
Sparse Core Ops, SparseCore 0:
  9.1 25.8 all-gather.1
  93.4 92.5 reduce-scatter.2
  241.7 31.5 reduce-scatter.4
